TPU v7x, 32 devices: a whole 2x2x4 slice. The times are simulated.
32 devices in a mesh: members: 2 (over y), tiles: 4 (over z), chan: 2 (over x), dirs: 2 (over core).
Axes of the slice: x: 2, y: 2, z: 4, core: 2. Of those that a mesh axis runs over, the one named last changes fastest.
Arguments:
- field: float32 [64, 128, 256], P(('members', 'tiles'), 'chan'), parts along dimension 0, may hold values from -6 to 6
- tangents: float32 [4, 64, 128, 256], P('dirs', ('members', 'tiles'), 'chan'), parts along dimension 1, may hold values from -6 to 6
- weight_one: float32 [9, 128, 128], replicated, may hold values from -0.1875 to 0.1875
- bias_one: float32 [128], replicated, may hold values from -3 to 3
- weight_two: float32 [9, 128, 128], replicated, may hold values from -0.1875 to 0.1875
- bias_two: float32 [128], replicated, may hold values from -3 to 3
- adjacency: int32 [32, 4], replicated, may hold values from 0 to 31
- side_code: int32 [32, 4], replicated, may hold values from 0 to 3
- mirror_flag: int32 [32, 4], replicated, may hold values from 0 to 1
- placement: int32 [32], replicated, may hold values from 0 to 31, each once
Outputs:
- output: float32 [64, 128, 256], P(('members', 'tiles'), 'chan'), parts along dimension 0
- output_tangents: float32 [4, 64, 128, 256], P('dirs', ('members', 'tiles'), 'chan'), parts along dimension 1
There are 2 independent parts, one for each index of `members`. A program takes and returns all parts, laid end to end along the dimension named above; an argument that names none is the same for every part. Nothing has to cross between parts.
Inputs may be any that keep to these rules, and one draw needn't show every extreme that they name: `adjacency`: tile ids; a tile may border itself or the same tile on several sides. `placement`: every tile id once.
All inputs are finite; a program needn't handle non-finite values.
Results may differ from a plain program's by a relative error of at most 0.00011.
Values sent between devices are 32-bit elements; how exact they have to be, the bound alone decides.
No kernel may reach another device: no remote copies, remote signals or barrier semaphores. Data moves between devices by JAX's collectives and lax.ppermute only.
A program may use at most 128 MiB of HBM per device.

v0:
```python
import jax
import jax.numpy as jnp
import numpy as np
from jax import lax
from jax.sharding import PartitionSpec as P

S = 16


def static_tables():
    width = S + 2
    length = width * width + 2
    where_at = np.arange(length)
    row_at = where_at // width
    col_at = where_at % width
    inside = where_at < width * width
    mid_row = (row_at >= 1) & (row_at <= S)
    mid_col = (col_at >= 1) & (col_at <= S)
    side_at = np.full(length, 4)
    along = np.zeros(length, dtype=np.int64)
    side_at = np.where(inside & (row_at == 0) & mid_col, 0, side_at)
    side_at = np.where(inside & (row_at == S + 1) & mid_col, 1, side_at)
    side_at = np.where(inside & (col_at == 0) & mid_row, 2, side_at)
    side_at = np.where(inside & (col_at == S + 1) & mid_row, 3, side_at)
    side_at = np.where(inside & mid_row & mid_col, -1, side_at)
    along = np.where((side_at == 0) | (side_at == 1), col_at - 1, along)
    along = np.where((side_at == 2) | (side_at == 3), row_at - 1, along)
    along = np.where(side_at == -1, (row_at - 1) * S + (col_at - 1), along)
    return (side_at.astype(np.int32), along.astype(np.int32))


def pad_index(flips):
    side_np, along_np = static_tables()
    side_at = jnp.asarray(side_np)
    along = jnp.asarray(along_np)
    side_safe = jnp.clip(side_at, 0, 3)
    flip_at = jnp.take(flips, side_safe, axis=1)
    rim_index = (
        S * S
        + side_safe[None, :] * S
        + jnp.where(flip_at == 1, S - 1 - along[None, :], along[None, :])
    )
    zero_index = S * S + 4 * S
    index = jnp.where(
        side_at[None, :] == -1,
        along[None, :],
        jnp.where(side_at[None, :] == 4, zero_index, rim_index),
    )
    return index.astype(jnp.int32)


def convolve(padded, weight):
    tap_count = weight.shape[0]
    out_count = weight.shape[1]
    width = S + 2
    span = S * width
    flat_weight = weight.reshape(tap_count * out_count, weight.shape[2])
    planes = jnp.einsum("kc,btcl->btkl", flat_weight, padded, precision=lax.Precision.HIGHEST)
    planes = planes.reshape(padded.shape[0], padded.shape[1], tap_count, out_count, padded.shape[3])
    summed = None
    for row_off in range(3):
        for col_off in range(3):
            offset = row_off * width + col_off
            term = planes[:, :, row_off * 3 + col_off, :, offset : offset + span]
            summed = term if summed is None else summed + term
    keep_np = (np.arange(S)[:, None] * width + np.arange(S)[None, :]).reshape(-1).astype(np.int32)
    return jnp.take(summed, jnp.asarray(keep_np), axis=-1)


def pad_fields(fields, near_slot, codes, index):
    stream_count = fields.shape[0]
    tile_count = fields.shape[1]
    chan_count = fields.shape[2]
    grid_view = fields.reshape(stream_count, tile_count, chan_count, S, S)
    edges = jnp.stack(
        [
            grid_view[..., 0, :],
            grid_view[..., S - 1, :],
            grid_view[..., :, 0],
            grid_view[..., :, S - 1],
        ],
        axis=2,
    )
    everyone = lax.all_gather(
        edges.reshape(stream_count, tile_count, 4 * chan_count * S), "tiles", axis=1, tiled=True
    )
    flat_edges = everyone.reshape(stream_count, everyone.shape[1] * 4, chan_count * S)
    lookup = (near_slot * 4 + codes).reshape(-1)
    rims = jnp.take(flat_edges, lookup, axis=1).reshape(stream_count, tile_count, 4, chan_count, S)
    rims = jnp.transpose(rims, (0, 1, 3, 2, 4)).reshape(stream_count, tile_count, chan_count, 4 * S)
    zeros_col = jnp.zeros((stream_count, tile_count, chan_count, 1), jnp.float32)
    source = jnp.concatenate([fields, rims, zeros_col], axis=-1)
    return jnp.take_along_axis(source, index[None, :, None, :], axis=-1)


def layer_sums(padded, weight):
    chan_group = padded.shape[2]
    chan_start = lax.axis_index("chan") * chan_group
    weight_rows = lax.dynamic_slice_in_dim(weight, chan_start, chan_group, 1)
    gathered = lax.all_gather(padded, "chan", axis=2, tiled=True)
    return convolve(gathered, weight_rows)


def local(
    field,
    tangents,
    weight_one,
    bias_one,
    weight_two,
    bias_two,
    adjacency,
    side_code,
    mirror_flag,
    placement,
):
    tile_count = field.shape[0]
    chan_group = field.shape[1]
    total_tiles = placement.shape[0]
    ident = jnp.arange(total_tiles, dtype=jnp.int32)
    slot_of = jnp.sum(jnp.where(placement[None, :] == ident[:, None], ident[None, :], 0), axis=1)
    mine = lax.dynamic_slice_in_dim(placement, lax.axis_index("tiles") * tile_count, tile_count)
    near_slot = jnp.take(slot_of, jnp.take(adjacency, mine, axis=0).reshape(-1), axis=0).reshape(
        tile_count, 4
    )
    codes = jnp.take(side_code, mine, axis=0)
    flips = jnp.take(mirror_flag, mine, axis=0)
    index = pad_index(flips)
    chan_start = lax.axis_index("chan") * chan_group
    streams = jnp.concatenate([field[None], tangents], axis=0)
    weights = (weight_one, weight_two)
    biases = (
        lax.dynamic_slice_in_dim(bias_one, chan_start, chan_group),
        lax.dynamic_slice_in_dim(bias_two, chan_start, chan_group),
    )
    result = None
    for layer in range(2):
        summed = layer_sums(pad_fields(streams, near_slot, codes, index), weights[layer])
        pre = summed[0] + biases[layer][:, None]
        if layer == 0:
            sigma = jax.nn.sigmoid(pre)
            slope = sigma * (1.0 + pre * (1.0 - sigma))
            streams = jnp.concatenate([(pre * sigma)[None], summed[1:] * slope[None]], axis=0)
        else:
            result = (pre, summed[1:])
    return result


def solution(mesh):
    placed = (
        P(("members", "tiles"), "chan", None),
        P("dirs", ("members", "tiles"), "chan", None),
        P(),
        P(),
        P(),
        P(),
        P(),
        P(),
        P(),
        P(),
    )
    return jax.shard_map(
        local,
        mesh=mesh,
        in_specs=placed,
        out_specs=(
            P(("members", "tiles"), "chan", None),
            P("dirs", ("members", "tiles"), "chan", None),
        ),
        check_vma=False,
    )
```

profile of v0, /device:TPU:0, one launch (start us, length us, event | category | flops | bytes accessed | tf_op | source)
XLA Modules:
  0.0 596.3 jit_solution(17269689504091182904)
XLA Ops:
  28.4 30.6 %all-gather.5.cloned.1.call-done = f32[3,32,4096]{2,1,0:T(8,128)} async-done(((f32[3,8,4096]{2,1,0:T(8,128)}), f32[3,32,4096]{2,1,0:T(8,128)}) %all-gather.5.cloned.1.call-update) | async-done | bytes 1572880 | tf_op jit(solution)/shard_map/all_gather | solution.py:84
  71.6 6.8 %maximum_maximum_fusion = f32[3,8,64,321]{2,0,3,1:T(4,128)} fusion(f32[3,8,64,64]{2,0,3,1:T(4,128)S(1)} %copy.267, f32[3,8,64,256]{2,0,3,1:T(4,128)} %copy.266, f32[321]{0:T(512)S(1)} %pad.10.clone), kind=kLoop, calls=%fused_computation.13 | loop fusion | flops 986112 | bytes 3939588 | tf_op jit(solution)/shard_map/concatenate | solution.py:92
  78.4 29.1 %gather_fusion.6 = f32[2608,3,64]{2,1,0:T(4,128)} fusion(f32[3,8,64,321]{2,0,3,1:T(4,128)} %maximum_maximum_fusion, s32[2608]{0:T(1024)S(1)} %reshape.450), kind=kCustom, calls=%fused_computation.2.clone | custom fusion | bytes 4026752 | tf_op jit(solution)/shard_map/jit(take_along_axis)/gather | solution.py:93
  107.5 5.1 copy.269
  114.5 61.5 %all-gather.7.cloned.1.call-done = f32[3,8,128,326]{3,2,1,0:T(8,128)} async-done(((f32[3,8,64,326]{3,2,1,0:T(8,128)}), f32[3,8,128,326]{3,2,1,0:T(8,128)}) %all-gather.7.cloned.1.call-update) | async-done | bytes 4005904 | tf_op jit(solution)/shard_map/all_gather | solution.py:100
  176.0 26.3 %convolution_bitcast_fusion.1 = f32[3,8,576,326]{2,3,1,0:T(8,128)} fusion(f32[3,8,128,326]{3,2,1,0:T(8,128)} %all-gather.7.cloned.1.call-done, f32[576,128,1,1]{1,0,3,2:T(8,128)S(1)} %bitcast.119), kind=kOutput, calls=%fused_computation.12 | convolution fusion | flops 6922174464 | bytes 22327296 | tf_op jit(solution)/shard_map/kc,btcl->btkl/dot_general | solution.py:58
  202.3 22.3 %copy.270 = f32[3,8,576,326]{3,2,1,0:T(8,128)} copy(f32[3,8,576,326]{2,3,1,0:T(8,128)} %convolution_bitcast_fusion.1) | data formatting | bytes 36052992 | tf_op jit(solution)/shard_map/kc,btcl->btkl/transpose | solution.py:58
  224.6 13.3 %fusion.4 = (f32[3,8,1,64,288]{4,3,2,1,0:T(8,128)}, f32[3,8,1,64,288]{4,3,2,1,0:T(8,128)}, f32[3,8,1,64,288]{4,3,2,1,0:T(8,128)}, f32[3,8,1,64,288]{4,3,2,1,0:T(...) fusion(f32[3,8,9,64,326]{4,3,2,1,0:T(8,128)} %bitcast.99), kind=kLoop, calls=%fused_computation.64 | loop fusion | bytes 31850496 | tf_op jit(solution)/shard_map/slice | solution.py:64
  237.9 4.7 copy.313
  242.6 4.7 copy.314
  247.2 4.7 copy.315
  251.9 4.7 copy.316
  256.6 4.7 copy.317
  261.3 4.7 copy.318
  266.0 4.7 copy.319
  270.7 4.7 copy.320
  278.7 12.7 %add_bitcast_fusion.1 = f32[3,8,64,288]{2,1,3,0:T(8,128)} fusion(f32[3,8,1,64,288]{3,1,4,0,2:T(8,128)} %copy.321, f32[3,8,1,64,288]{3,1,4,0,2:T(8,128)} %copy.320, f32[3,8,1,64,288]{3,1,4,0,2:T(8,128)} %copy.319, f32[3,8,1,64,288]{3,1,4,0,2:T(8,128)} %copy.318, f32[3,8,1,64,288]{3,1,4,0,2:T(8,128)} %copy.317, f32[3,8,1,64,288]{3,1,4,0,2:T(8,128)} %copy.316, ...), kind=kLoop, calls=%fused_computation.16 | loop fusion | flops 3538944 | bytes 17694720 | tf_op jit(solution)/shard_map/add | solution.py:65
  307.5 37.1 %all-gather.9.cloned.1.call-done = f32[3,32,4096]{2,1,0:T(8,128)} async-done(((f32[3,8,4096]{2,1,0:T(8,128)}), f32[3,32,4096]{2,1,0:T(8,128)}) %all-gather.9.cloned.1.call-update) | async-done | bytes 1572880 | tf_op jit(solution)/shard_map/all_gather | solution.py:84
  365.7 29.3 %gather_fusion.9 = f32[2608,3,64]{2,1,0:T(4,128)} fusion(f32[3,8,64,321]{2,0,3,1:T(4,128)} %copy.290, s32[2608]{0:T(1024)S(1)} %reshape.450), kind=kCustom, calls=%fused_computation.7.clone | custom fusion | bytes 4026752 | tf_op jit(solution)/shard_map/jit(take_along_axis)/gather | solution.py:93
  395.1 4.9 copy.292
  401.8 61.5 %all-gather.11.cloned.1.call-done = f32[3,8,128,326]{3,2,1,0:T(8,128)} async-done(((f32[3,8,64,326]{3,2,1,0:T(8,128)}), f32[3,8,128,326]{3,2,1,0:T(8,128)}) %all-gather.11.cloned.1.call-update) | async-done | bytes 4005904 | tf_op jit(solution)/shard_map/all_gather | solution.py:100
  463.3 26.3 %convolution_bitcast_fusion = f32[3,8,576,326]{2,3,1,0:T(8,128)} fusion(f32[3,8,128,326]{3,2,1,0:T(8,128)} %all-gather.11.cloned.1.call-done, f32[576,128,1,1]{1,0,3,2:T(8,128)S(1)} %bitcast.118), kind=kOutput, calls=%fused_computation.11 | convolution fusion | flops 6922174464 | bytes 22327296 | tf_op jit(solution)/shard_map/kc,btcl->btkl/dot_general | solution.py:58
  489.6 22.3 %copy.293 = f32[3,8,576,326]{3,2,1,0:T(8,128)} copy(f32[3,8,576,326]{2,3,1,0:T(8,128)} %convolution_bitcast_fusion) | data formatting | bytes 36052992 | tf_op jit(solution)/shard_map/kc,btcl->btkl/transpose | solution.py:58
  511.9 13.3 %fusion.3 = (f32[3,8,1,64,288]{4,3,2,1,0:T(8,128)}, f32[3,8,1,64,288]{4,3,2,1,0:T(8,128)}, f32[3,8,1,64,288]{4,3,2,1,0:T(8,128)}, f32[3,8,1,64,288]{4,3,2,1,0:T(...) fusion(f32[3,8,9,64,326]{4,3,2,1,0:T(8,128)} %bitcast.100), kind=kLoop, calls=%fused_computation.63 | loop fusion | bytes 31850496 | tf_op jit(solution)/shard_map/slice | solution.py:64
  525.1 4.7 copy.322
  529.8 4.7 copy.323
  539.2 4.7 copy.325
  543.9 4.7 copy.326
  548.6 4.7 copy.327
  553.3 4.7 copy.328
  558.0 4.9 copy.329
  566.0 12.7 %add_bitcast_fusion = f32[3,8,64,288]{2,1,3,0:T(8,128)} fusion(f32[3,8,1,64,288]{3,1,4,0,2:T(8,128)} %copy.330, f32[3,8,1,64,288]{3,1,4,0,2:T(8,128)} %copy.329, f32[3,8,1,64,288]{3,1,4,0,2:T(8,128)} %copy.328, f32[3,8,1,64,288]{3,1,4,0,2:T(8,128)} %copy.327, f32[3,8,1,64,288]{3,1,4,0,2:T(8,128)} %copy.326, f32[3,8,1,64,288]{3,1,4,0,2:T(8,128)} %copy.325, ...), kind=kLoop, calls=%fused_computation.15 | loop fusion | flops 3538944 | bytes 17694720 | tf_op jit(solution)/shard_map/add | solution.py:65
  (130 shorter events, 96.0 us)
Async XLA Ops:
  7.2 107.3 %copy-start = (f32[9,128,128]{2,1,0:T(8,128)S(1)}, f32[9,128,128]{2,1,0:T(8,128)}, u32[]{:S(2)}) copy-start(f32[9,128,128]{2,1,0:T(8,128)} %param.24) | copy-start | bytes 1769476
  7.2 2.0 copy-start.6
  7.2 51.8 %all-gather.5.cloned.1.call-start = ((), (), s32[]{:S(2)}) async-start(), calls=%async_computation | async-start | bytes 1966080 | tf_op jit(solution)/shard_map/all_gather | solution.py:84
  10.5 1.6 copy-start.2
  12.2 6.9 %copy-start.13 = (s32[32,4]{0,1:T(4,128)S(1)}, s32[32,4]{0,1:T(4,128)}, u32[]{:S(2)}) copy-start(s32[32,4]{0,1:T(4,128)} %param.28) | copy-start | bytes 1540
  12.3 7.0 %copy-start.14 = (s32[32,4]{0,1:T(4,128)S(1)}, s32[32,4]{0,1:T(4,128)}, u32[]{:S(2)}) copy-start(s32[32,4]{0,1:T(4,128)} %param.30) | copy-start | bytes 1540
  12.3 7.0 %copy-start.18 = (s32[32]{0:T(128)S(1)}, s32[32]{0:T(128)}, u32[]{:S(2)}) copy-start(s32[32]{0:T(128)} %param.31) | copy-start | bytes 388
  12.3 8.4 %copy-start.17 = (s32[256]{0:T(256)S(1)}, s32[256]{0:T(256)}, u32[]{:S(2)}) copy-start(s32[256]{0:T(256)} %constant.181) | copy-start | bytes 3076
  14.5 7.1 %copy-start.15 = (s32[32,4]{0,1:T(4,128)S(1)}, s32[32,4]{0,1:T(4,128)}, u32[]{:S(2)}) copy-start(s32[32,4]{0,1:T(4,128)} %param.29) | copy-start | bytes 1540
  14.5 7.9 %copy-start.5 = (f32[2,8,64,256]{3,2,1,0:T(8,128)S(1)}, f32[2,8,64,256]{3,2,1,0:T(8,128)}, u32[]{:S(2)}) copy-start(f32[2,8,64,256]{3,2,1,0:T(8,128)} %param.23) | copy-start | bytes 3145732
  19.1 156.9 %all-gather.7.cloned.1.call-start = ((), (), s32[]{:S(2)}) async-start(), calls=%async_computation.1 | async-start | bytes 7077888 | tf_op jit(solution)/shard_map/all_gather | solution.py:100
  23.6 3.3 copy-start.16
  23.6 4.4 copy-start.8
  23.6 4.4 copy-start.9
  23.6 4.4 copy-start.10
  23.7 4.4 copy-start.11
  23.7 4.4 copy-start.12
  112.7 1.7 copy-start.19
  114.4 230.2 %all-gather.9.cloned.1.call-start = ((), (), s32[]{:S(2)}) async-start(), calls=%async_computation.2 | async-start | bytes 1966080 | tf_op jit(solution)/shard_map/all_gather | solution.py:84
  296.0 2.2 copy-start.4
  297.7 1.3 copy-start.3
  307.4 155.9 %all-gather.11.cloned.1.call-start = ((), (), s32[]{:S(2)}) async-start(), calls=%async_computation.3 | async-start | bytes 7077888 | tf_op jit(solution)/shard_map/all_gather | solution.py:100
  400.0 1.7 copy-start.20
  400.0 1.8 copy-start.7
  583.3 6.3 %copy-start.1 = (f32[9,128,128]{2,1,0:T(8,128)S(1)}, f32[9,128,128]{2,1,0:T(8,128)}, u32[]{:S(2)}) copy-start(f32[9,128,128]{2,1,0:T(8,128)} %param.24) | copy-start | bytes 1769476
Sparse Core Ops, SparseCore 0:
  19.2 39.7 all-gather.4
  114.5 61.4 all-gather.6
  307.5 37.0 all-gather.8
  401.8 61.4 all-gather.10
where the time goes:
time: 607 us; the launch traced here: 596 us
  local copies, waits for them, and re-layouts  293 us (48%)
  waiting for transfers between devices  191 us (31%)
  matrix products  52.6 us (9%)
  other arithmetic  45.5 us (7%)
  between operations  14.5 us (2%)
    all_gather x2, waiting for transfers between devices, layer_sums(): gathered = lax.all_gather(padded, 'chan', axis=2, tiled=True)  123 us
    unnamed x68, local copies, waits for them, and re-layouts  89.5 us
    gather x5, local copies, waits for them, and re-layouts, pad_fields(): return jnp.take_along_axis(source, index[None, :, None, :], axis=-1)  68.6 us
    all_gather x2, waiting for transfers between devices, pad_fields(): lax.all_gather(edges.reshape(stream_count, tile_count, 4 * chan_count * S...  67.7 us
    dot_general x2, matrix products, convolve(): jnp.einsum('kc,btcl->btkl', flat_weight, padded, precision=lax.Precision....  52.6 us
    transpose x2, local copies, waits for them, and re-layouts, convolve(): jnp.einsum('kc,btcl->btkl', flat_weight, padded, precision=lax.Precision....  44.5 us
    slice x2, local copies, waits for them, and re-layouts, convolve(): term = planes[:, :, row_off * 3 + col_off, :, offset:offset + span]  26.5 us
    add x2, other arithmetic, convolve(): summed = term if summed is None else summed + term  25.5 us
  transfers between devices with their start and end apart: 4, of which 4 were waited for; matrix products, arithmetic and copies ran while one was open for 2% of the time, Pallas kernels for 0%

commit v1 on v0

--- a/solution.py
+++ b/solution.py
@@ -97,7 +97,7 @@
     chan_group = padded.shape[2]
     chan_start = lax.axis_index("chan") * chan_group
     weight_rows = lax.dynamic_slice_in_dim(weight, chan_start, chan_group, 1)
-    gathered = lax.all_gather(padded, "chan", axis=2, tiled=True)
+    gathered = jnp.concatenate(lax.all_gather(padded, "chan"), axis=2)
     return convolve(gathered, weight_rows)
 
 

time: 607 us -> 610 us (level)
  no operation moved by 1% of the time
where the time goes in v1:
time: 610 us; the launch traced here: 600 us
  local copies, waits for them, and re-layouts  299 us (49%)
  waiting for transfers between devices  191 us (31%)
  matrix products  50.6 us (8%)
  other arithmetic  44 us (7%)
  between operations  14.5 us (2%)
    all_gather x2, waiting for transfers between devices, layer_sums(): gathered = jnp.concatenate(lax.all_gather(padded, 'chan'), axis=2)  123 us
    unnamed x68, local copies, waits for them, and re-layouts  89.3 us
    all_gather x2, waiting for transfers between devices, pad_fields(): lax.all_gather(edges.reshape(stream_count, tile_count, 4 * chan_count * S...  67.7 us
    gather x5, local copies, waits for them, and re-layouts, pad_fields(): return jnp.take_along_axis(source, index[None, :, None, :], axis=-1)  67.7 us
    dot_general x2, matrix products, convolve(): jnp.einsum('kc,btcl->btkl', flat_weight, padded, precision=lax.Precision....  50.6 us
    transpose x2, local copies, waits for them, and re-layouts, convolve(): jnp.einsum('kc,btcl->btkl', flat_weight, padded, precision=lax.Precision....  44.5 us
    slice x2, local copies, waits for them, and re-layouts, convolve(): term = planes[:, :, row_off * 3 + col_off, :, offset:offset + span]  26.8 us
    add x2, other arithmetic, convolve(): summed = term if summed is None else summed + term  25.5 us
  transfers between devices with their start and end apart: 4, of which 4 were waited for; matrix products, arithmetic and copies ran while one was open for 2% of the time, Pallas kernels for 0%

profile of v1, /device:TPU:0, one launch (start us, length us, event | category | flops | bytes accessed | tf_op | source)
XLA Modules:
  0.0 599.6 jit_solution(16407415747729645946)
XLA Ops:
  28.4 30.6 %all-gather.7.cloned.1.call-done = f32[3,32,4096]{2,1,0:T(8,128)} async-done(((f32[3,8,4096]{2,1,0:T(8,128)}), f32[3,32,4096]{2,1,0:T(8,128)}) %all-gather.7.cloned.1.call-update) | async-done | bytes 1572880 | tf_op jit(solution)/shard_map/all_gather | solution.py:84
  71.6 6.8 %maximum_maximum_fusion = f32[3,8,64,321]{2,0,3,1:T(4,128)} fusion(f32[3,8,64,64]{2,0,3,1:T(4,128)S(1)} %copy.279, f32[3,8,64,256]{2,0,3,1:T(4,128)} %copy.278, f32[321]{0:T(512)S(1)} %pad.10.clone), kind=kLoop, calls=%fused_computation.13 | loop fusion | flops 986112 | bytes 3939588 | tf_op jit(solution)/shard_map/concatenate | solution.py:92
  78.4 29.1 %gather_fusion.6 = f32[2608,3,64]{2,1,0:T(4,128)} fusion(f32[3,8,64,321]{2,0,3,1:T(4,128)} %maximum_maximum_fusion, s32[2608]{0:T(1024)S(1)} %reshape.468), kind=kCustom, calls=%fused_computation.2.clone | custom fusion | bytes 4026752 | tf_op jit(solution)/shard_map/jit(take_along_axis)/gather | solution.py:93
  107.5 5.1 copy.280
  114.5 61.5 %all-gather.11.cloned.1.call-done = f32[6,8,64,326]{3,2,1,0:T(8,128)} async-done(((f32[3,8,64,326]{3,2,1,0:T(8,128)}), f32[6,8,64,326]{3,2,1,0:T(8,128)}) %all-gather.11.cloned.1.call-update) | async-done | bytes 4005904 | tf_op jit(solution)/shard_map/all_gather | solution.py:100
  178.9 25.3 %convolution_bitcast_fusion.1 = f32[3,8,576,326]{2,3,1,0:T(8,128)} fusion(f32[3,8,128,326]{3,2,1,0:T(8,128)S(1)} %bitcast.112, f32[576,128,1,1]{1,0,3,2:T(8,128)S(1)} %bitcast.131), kind=kOutput, calls=%fused_computation.12 | convolution fusion | flops 6922174464 | bytes 22327296 | tf_op jit(solution)/shard_map/kc,btcl->btkl/dot_general | solution.py:58
  204.2 22.3 %copy.283 = f32[3,8,576,326]{3,2,1,0:T(8,128)} copy(f32[3,8,576,326]{2,3,1,0:T(8,128)} %convolution_bitcast_fusion.1) | data formatting | bytes 36052992 | tf_op jit(solution)/shard_map/kc,btcl->btkl/transpose | solution.py:58
  226.4 13.3 %fusion.4 = (f32[3,8,1,64,288]{4,3,2,1,0:T(8,128)}, f32[3,8,1,64,288]{4,3,2,1,0:T(8,128)}, f32[3,8,1,64,288]{4,3,2,1,0:T(8,128)}, f32[3,8,1,64,288]{4,3,2,1,0:T(...) fusion(f32[3,8,9,64,326]{4,3,2,1,0:T(8,128)} %bitcast.107), kind=kLoop, calls=%fused_computation.64 | loop fusion | bytes 31850496 | tf_op jit(solution)/shard_map/slice | solution.py:64
  239.7 4.7 copy.327
  244.4 4.7 copy.328
  249.1 4.7 copy.329
  253.7 4.8 copy.330
  258.6 4.7 copy.331
  263.3 4.7 copy.332
  268.0 4.7 copy.333
  272.7 4.7 copy.334
  280.5 12.7 %add_bitcast_fusion.1 = f32[3,8,64,288]{2,1,3,0:T(8,128)} fusion(f32[3,8,1,64,288]{3,1,4,0,2:T(8,128)} %copy.335, f32[3,8,1,64,288]{3,1,4,0,2:T(8,128)} %copy.334, f32[3,8,1,64,288]{3,1,4,0,2:T(8,128)} %copy.333, f32[3,8,1,64,288]{3,1,4,0,2:T(8,128)} %copy.332, f32[3,8,1,64,288]{3,1,4,0,2:T(8,128)} %copy.331, f32[3,8,1,64,288]{3,1,4,0,2:T(8,128)} %copy.330, ...), kind=kLoop, calls=%fused_computation.16 | loop fusion | flops 3538944 | bytes 17694720 | tf_op jit(solution)/shard_map/add | solution.py:65
  309.3 37.1 %all-gather.9.cloned.1.call-done = f32[3,32,4096]{2,1,0:T(8,128)} async-done(((f32[3,8,4096]{2,1,0:T(8,128)}), f32[3,32,4096]{2,1,0:T(8,128)}) %all-gather.9.cloned.1.call-update) | async-done | bytes 1572880 | tf_op jit(solution)/shard_map/all_gather | solution.py:84
  367.6 29.3 %gather_fusion.9 = f32[2608,3,64]{2,1,0:T(4,128)} fusion(f32[3,8,64,321]{2,0,3,1:T(4,128)} %copy.303, s32[2608]{0:T(1024)S(1)} %reshape.468), kind=kCustom, calls=%fused_computation.7.clone | custom fusion | bytes 4026752 | tf_op jit(solution)/shard_map/jit(take_along_axis)/gather | solution.py:93
  403.2 61.5 %all-gather.13.cloned.1.call-done = f32[6,8,64,326]{3,2,1,0:T(8,128)} async-done(((f32[3,8,64,326]{3,2,1,0:T(8,128)}), f32[6,8,64,326]{3,2,1,0:T(8,128)}) %all-gather.13.cloned.1.call-update) | async-done | bytes 4005904 | tf_op jit(solution)/shard_map/all_gather | solution.py:100
  467.6 25.3 %convolution_bitcast_fusion = f32[3,8,576,326]{2,3,1,0:T(8,128)} fusion(f32[3,8,128,326]{3,2,1,0:T(8,128)S(1)} %bitcast.113, f32[576,128,1,1]{1,0,3,2:T(8,128)S(1)} %bitcast.130), kind=kOutput, calls=%fused_computation.11 | convolution fusion | flops 6922174464 | bytes 22327296 | tf_op jit(solution)/shard_map/kc,btcl->btkl/dot_general | solution.py:58
  492.8 22.3 %copy.308 = f32[3,8,576,326]{3,2,1,0:T(8,128)} copy(f32[3,8,576,326]{2,3,1,0:T(8,128)} %convolution_bitcast_fusion) | data formatting | bytes 36052992 | tf_op jit(solution)/shard_map/kc,btcl->btkl/transpose | solution.py:58
  515.1 13.5 %fusion.3 = (f32[3,8,1,64,288]{4,3,2,1,0:T(8,128)}, f32[3,8,1,64,288]{4,3,2,1,0:T(8,128)}, f32[3,8,1,64,288]{4,3,2,1,0:T(8,128)}, f32[3,8,1,64,288]{4,3,2,1,0:T(...) fusion(f32[3,8,9,64,326]{4,3,2,1,0:T(8,128)} %bitcast.108), kind=kLoop, calls=%fused_computation.63 | loop fusion | bytes 31850496 | tf_op jit(solution)/shard_map/slice | solution.py:64
  528.6 4.7 copy.336
  533.3 4.7 copy.337
  538.0 4.7 copy.338
  542.6 4.7 copy.339
  547.3 4.7 copy.340
  552.0 4.7 copy.341
  556.7 4.7 copy.342
  561.5 4.7 copy.343
  569.2 12.7 %add_bitcast_fusion = f32[3,8,64,288]{2,1,3,0:T(8,128)} fusion(f32[3,8,1,64,288]{3,1,4,0,2:T(8,128)} %copy.344, f32[3,8,1,64,288]{3,1,4,0,2:T(8,128)} %copy.343, f32[3,8,1,64,288]{3,1,4,0,2:T(8,128)} %copy.342, f32[3,8,1,64,288]{3,1,4,0,2:T(8,128)} %copy.341, f32[3,8,1,64,288]{3,1,4,0,2:T(8,128)} %copy.340, f32[3,8,1,64,288]{3,1,4,0,2:T(8,128)} %copy.339, ...), kind=kLoop, calls=%fused_computation.15 | loop fusion | flops 3538944 | bytes 17694720 | tf_op jit(solution)/shard_map/add | solution.py:65
  (133 shorter events, 101.3 us)
Async XLA Ops:
  7.2 107.3 %copy-start = (f32[9,128,128]{2,1,0:T(8,128)S(1)}, f32[9,128,128]{2,1,0:T(8,128)}, u32[]{:S(2)}) copy-start(f32[9,128,128]{2,1,0:T(8,128)} %param.24) | copy-start | bytes 1769476
  7.2 2.0 copy-start.6
  7.2 51.8 %all-gather.7.cloned.1.call-start = ((), (), s32[]{:S(2)}) async-start(), calls=%async_computation | async-start | bytes 1966080 | tf_op jit(solution)/shard_map/all_gather | solution.py:84
  10.5 1.6 copy-start.2
  12.2 6.9 %copy-start.13 = (s32[32,4]{0,1:T(4,128)S(1)}, s32[32,4]{0,1:T(4,128)}, u32[]{:S(2)}) copy-start(s32[32,4]{0,1:T(4,128)} %param.28) | copy-start | bytes 1540
  12.3 7.0 %copy-start.14 = (s32[32,4]{0,1:T(4,128)S(1)}, s32[32,4]{0,1:T(4,128)}, u32[]{:S(2)}) copy-start(s32[32,4]{0,1:T(4,128)} %param.30) | copy-start | bytes 1540
  12.3 7.0 %copy-start.18 = (s32[32]{0:T(128)S(1)}, s32[32]{0:T(128)}, u32[]{:S(2)}) copy-start(s32[32]{0:T(128)} %param.31) | copy-start | bytes 388
  12.3 8.4 %copy-start.17 = (s32[256]{0:T(256)S(1)}, s32[256]{0:T(256)}, u32[]{:S(2)}) copy-start(s32[256]{0:T(256)} %constant.181) | copy-start | bytes 3076
  14.5 7.1 %copy-start.15 = (s32[32,4]{0,1:T(4,128)S(1)}, s32[32,4]{0,1:T(4,128)}, u32[]{:S(2)}) copy-start(s32[32,4]{0,1:T(4,128)} %param.29) | copy-start | bytes 1540
  14.5 7.9 %copy-start.5 = (f32[2,8,64,256]{3,2,1,0:T(8,128)S(1)}, f32[2,8,64,256]{3,2,1,0:T(8,128)}, u32[]{:S(2)}) copy-start(f32[2,8,64,256]{3,2,1,0:T(8,128)} %param.23) | copy-start | bytes 3145732
  19.1 156.9 %all-gather.11.cloned.1.call-start = ((), (), s32[]{:S(2)}) async-start(), calls=%async_computation.2 | async-start | bytes 7077888 | tf_op jit(solution)/shard_map/all_gather | solution.py:100
  23.6 3.3 copy-start.16
  23.6 4.4 copy-start.8
  23.6 4.4 copy-start.9
  23.6 4.4 copy-start.10
  23.7 4.4 copy-start.11
  23.7 4.4 copy-start.12
  112.7 1.7 copy-start.19
  114.4 232.1 %all-gather.9.cloned.1.call-start = ((), (), s32[]{:S(2)}) async-start(), calls=%async_computation.1 | async-start | bytes 1966080 | tf_op jit(solution)/shard_map/all_gather | solution.py:84
  297.8 2.2 copy-start.4
  299.6 1.3 copy-start.3
  309.2 155.4 %all-gather.13.cloned.1.call-start = ((), (), s32[]{:S(2)}) async-start(), calls=%async_computation.3 | async-start | bytes 7077888 | tf_op jit(solution)/shard_map/all_gather | solution.py:100
  401.1 1.9 copy-start.20
  401.2 2.0 copy-start.7
  586.5 6.3 %copy-start.1 = (f32[9,128,128]{2,1,0:T(8,128)S(1)}, f32[9,128,128]{2,1,0:T(8,128)}, u32[]{:S(2)}) copy-start(f32[9,128,128]{2,1,0:T(8,128)} %param.24) | copy-start | bytes 1769476
Sparse Core Ops, SparseCore 0:
  19.2 39.7 all-gather.6
  114.5 61.4 all-gather.10
  309.4 37.0 all-gather.8
  403.2 61.4 all-gather.12
